TPU v7x, 128 devices: a whole 4x4x4 slice. The times are simulated.
128 devices in a mesh: stripe: 32 (over x, y_lo, z), sub: 4 (over y_hi, core).
Axes of the slice: x: 4, y: 4 (y_hi: 2, y_lo: 2; y = y_hi * 2 + y_lo), z: 4, core: 2. Of those that a mesh axis runs over, the one named last changes fastest.
Arguments:
- channel: float32 [8, 32, 64, 512], P('sub', 'stripe'), may hold values from -0.25 to 0.25
- received: float32 [8, 32, 2048], P('sub', None, 'stripe'), may hold values from -18 to 18
- noise_var: float32 [8, 32], P('sub', 'stripe'), may hold values from 0.25 to 4
- downlink: float32 [8, 32, 512], P('sub'), may hold values from -6 to 6
- user_order: int32 [512], P('stripe'), may hold values from 0 to 511, each once
Outputs:
- transmit: float32 [8, 32, 2048], P('sub', None, 'stripe')
- owned: float32 [8, 32, 512], P('sub', None, 'stripe')
Inputs may be any that keep to these rules, and one draw needn't show every extreme that they name: `user_order`: a permutation of the 512 users.
All inputs are finite; a program needn't handle non-finite values.
Results may differ from a plain program's by a relative error of at most 0.00017.
Values sent between devices are 32-bit elements; how exact they have to be, the bound alone decides.
No kernel may reach another device: no remote copies, remote signals or barrier semaphores. Data moves between devices by JAX's collectives and lax.ppermute only.
A program may use at most 256 MiB of HBM per device.

v0:
```python
import jax
import jax.numpy as jnp
from jax import lax
from jax.sharding import PartitionSpec as P

prior_var = 0.1


def from_behind(value, axis, steps):
    count = lax.axis_size(axis)
    first, last = (max(0, -steps), min(count, count - steps))
    return lax.ppermute(value, axis, [(source, source + steps) for source in range(first, last)])


def from_root(block, axis, source):
    block = jnp.where(lax.axis_index(axis) == source, block, jnp.zeros_like(block))
    return lax.psum(block, axis)


def product(left, right):
    return jnp.dot(left, right, precision=lax.Precision.HIGHEST, preferred_element_type=jnp.float32)


def woodbury(covariance, estimate, matrix, samples, variance):
    cross_term = product(covariance, matrix.T)
    system = product(matrix, cross_term) + variance * jnp.eye(matrix.shape[0], dtype=jnp.float32)
    factor = jnp.linalg.cholesky(system)
    gain_rows = jax.scipy.linalg.cho_solve((factor, True), cross_term.T)
    residual_rows = samples - product(estimate, matrix.T)
    estimate = estimate + product(residual_rows, gain_rows)
    covariance = covariance - product(cross_term, gain_rows)
    return (covariance, estimate)


def shards(channel, received, noise_var, downlink, user_order):
    local_blocks, local_links, antennas, user_count = channel.shape
    symbols = received.shape[1]
    samples = received.reshape(local_blocks, symbols, local_links, antennas).transpose(0, 2, 1, 3)
    eye_users = jnp.eye(user_count, dtype=jnp.float32)
    position = lax.axis_index("stripe")
    length = lax.axis_size("stripe")
    prior_cov = prior_var * eye_users
    prior_est = jnp.zeros((symbols, user_count), jnp.float32)

    def apply_links(covariance, estimate, block_index):
        matrices = lax.dynamic_index_in_dim(channel, block_index, 0, keepdims=False)
        sample_rows = lax.dynamic_index_in_dim(samples, block_index, 0, keepdims=False)
        variances = lax.dynamic_index_in_dim(noise_var, block_index, 0, keepdims=False)
        covariance, estimate = woodbury(
            covariance, estimate, matrices[0], sample_rows[0], variances[0]
        )
        return (covariance, estimate)

    def one_turn(turn_index, carried):
        out_cov, out_est, kept_cov, kept_est = carried
        in_cov, in_est = from_behind((out_cov, out_est), "stripe", 1)
        is_first = position == 0
        in_cov = jnp.where(is_first, prior_cov, in_cov)
        in_est = jnp.where(is_first, prior_est, in_est)
        block_index = turn_index - position
        is_valid = (block_index >= 0) & (block_index < local_blocks)
        clipped = jnp.clip(block_index, 0, local_blocks - 1)
        new_cov, new_est = apply_links(in_cov, in_est, clipped)
        keep_it = is_valid & (position == length - 1)
        old_cov = lax.dynamic_index_in_dim(kept_cov, clipped, 0, keepdims=False)
        old_est = lax.dynamic_index_in_dim(kept_est, clipped, 0, keepdims=False)
        kept_cov = lax.dynamic_update_index_in_dim(
            kept_cov, jnp.where(keep_it, new_cov, old_cov), clipped, 0
        )
        kept_est = lax.dynamic_update_index_in_dim(
            kept_est, jnp.where(keep_it, new_est, old_est), clipped, 0
        )
        return (new_cov, new_est, kept_cov, kept_est)

    initial = (
        prior_cov,
        prior_est,
        jnp.zeros((local_blocks, user_count, user_count), jnp.float32),
        jnp.zeros((local_blocks, symbols, user_count), jnp.float32),
    )
    carried = lax.fori_loop(0, local_blocks + length - 1, one_turn, initial)
    covars, estimates = (
        from_root(carried[2], "stripe", length - 1),
        from_root(carried[3], "stripe", length - 1),
    )
    diag_sum = jnp.sum(jnp.diagonal(covars, axis1=1, axis2=2), axis=0)
    total = lax.psum(diag_sum, "sub")
    mean_error = total / (local_blocks * lax.axis_size("sub"))
    power_scale = lax.rsqrt(mean_error)
    precoded = (
        jnp.einsum("bsk,bkn->bsn", downlink, covars, precision=lax.Precision.HIGHEST) * power_scale
    )
    transmit = jnp.einsum("bsk,blmk->bslm", precoded, channel, precision=lax.Precision.HIGHEST)
    transmit = transmit.reshape(local_blocks, symbols, local_links * antennas)
    owned_rows = jnp.take(estimates, user_order, axis=2)
    return (transmit, owned_rows)


def solution(mesh):
    return jax.shard_map(
        shards,
        mesh=mesh,
        in_specs=(
            P("sub", "stripe", None, None),
            P("sub", None, "stripe"),
            P("sub", "stripe"),
            P("sub", None, None),
            P("stripe"),
        ),
        out_specs=(P("sub", None, "stripe"), P("sub", None, "stripe")),
        check_vma=False,
    )
```

profile of v0, /device:TPU:1, one launch (start us, length us, event | category | flops | bytes accessed | tf_op | source)
XLA Modules:
  0.0 1959.1 jit_solution(15671876080877473592)
XLA Ops:
  9.3 1484.5 %while.21 = (s32[]{:T(128)}, f32[512,512]{1,0:T(8,128)}, f32[32,512]{1,0:T(8,128)S(1)}, f32[2,512,512]{2,1,0:T(8,128)S(1)}, f32[2,32,512]{2,1,0:T(8,128)}, /*ind...) while((s32[]{:T(128)}, f32[512,512]{1,0:T(8,128)}, ...), condition=%wide.region_3.4_spmd.clone, body=%wide.region_0.3_spmd.clone.sunk | while | flops 505559104 | bytes 14437732 | solution.py:81
  20.0 17.1 collective-permute-done.1
  59.2 6.8 collective-permute-start
  71.3 16.3 collective-permute-done.1
  93.3 6.6 cholesky.65
  109.7 6.8 collective-permute-start
  121.8 15.6 collective-permute-done.1
  159.5 6.8 collective-permute-start
  171.6 14.8 collective-permute-done.1
  192.1 6.6 cholesky.65
  208.5 6.8 collective-permute-start
  221.8 12.9 collective-permute-done.1
  256.8 7.1 collective-permute-start
  272.3 10.1 collective-permute-done.1
  304.4 9.2 collective-permute-start
  322.0 9.3 collective-permute-done.1
  353.4 9.2 collective-permute-start
  370.9 8.5 collective-permute-done.1
  401.6 9.3 collective-permute-start
  419.1 7.9 collective-permute-done.1
  449.1 9.1 collective-permute-start
  466.6 7.0 collective-permute-done.1
  495.7 9.3 collective-permute-start
  541.7 9.3 collective-permute-start
  587.0 9.3 collective-permute-start
  631.6 9.2 collective-permute-start
  675.3 9.3 collective-permute-start
  718.2 9.1 collective-permute-start
  761.0 9.3 collective-permute-start
  804.0 9.0 collective-permute-start
  846.7 8.9 collective-permute-start
  889.4 8.8 collective-permute-start
  931.9 10.1 collective-permute-start
  975.6 9.9 collective-permute-start
  1019.2 9.8 collective-permute-start
  1062.7 9.4 collective-permute-start
  1105.8 9.4 collective-permute-start
  1148.9 9.4 collective-permute-start
  1192.0 9.4 collective-permute-start
  1235.1 9.4 collective-permute-start
  1278.3 9.4 collective-permute-start
  1321.4 9.4 collective-permute-start
  1364.5 9.4 collective-permute-start
  1407.6 9.4 collective-permute-start
  1450.7 9.4 collective-permute-start
  1496.7 355.5 %all-reduce.3.cloned.1.call-done = (f32[2,512,512]{2,1,0:T(8,128)}, f32[2,32,512]{2,1,0:T(8,128)}) async-done(((f32[2,512,512]{2,1,0:T(8,128)}, f32[2,32,512]{2,1,0:T(8,128)}), (f32[2,512,512]{2,1,0:T(8,128)}, f32[2,32,512]{2,1,0:T(8,128)})) %all-reduce.3.cloned.1.call-update) | async-done | bytes 2228240 | tf_op jit(solution)/shard_map/psum | solution.py:17
  1854.7 60.2 %copy.23 = f32[2,512,512]{0,2,1:T(8,128)} copy(f32[2,512,512]{2,1,0:T(8,128)} %get-tuple-element.308) | data formatting | bytes 4194304 | tf_op jit(solution)/shard_map/psum | solution.py:17
  1920.6 28.3 %psum.22 = f32[512]{0:T(512)S(1)} all-reduce(f32[512]{0:T(512)S(1)} %reduce_sum.9), channel_id=1, replica_groups=mesh['stripe'=32,'sub'=4] {'sub'}, use_global_device_ids=true, to_apply=%region_6.7 | all-reduce | flops 512 | bytes 4096 | tf_op jit(solution)/shard_map/psum | solution.py:87
  (775 shorter events, 1078.1 us)
Async XLA Ops:
  7.2 1845.1 %all-reduce.3.cloned.1.call-start = ((), (), s32[]{:S(2)}) async-start(), calls=%async_computation | async-start | bytes 4456448 | tf_op jit(solution)/shard_map/psum | solution.py:17
  9.3 29.0 %collective-permute-start = (f32[512,512]{1,0:T(8,128)}, f32[512,512]{1,0:T(8,128)}, u32[]{:S(2)}, u32[]{:S(2)}) collective-permute-start(f32[512,512]{1,0:T(8,128)} %get-tuple-element.404), channel_id=1, source_target_pairs={{0,4},{4,8},{8,12},{12,16},{16,20},{20,24},{24,28},{28,32},{32,36}... | collective-permute-start | bytes 3145736 | tf_op jit(solution)/shard_map/while/body/eval_jaxpr/ppermute | solution.py:12
  14.7 22.4 %collective-permute-start.1 = (f32[32,512]{1,0:T(8,128)S(1)}, f32[32,512]{1,0:T(8,128)S(1)}, u32[]{:S(2)}, u32[]{:S(2)}) collective-permute-start(f32[32,512]{1,0:T(8,128)S(1)} %broadcast_select_fusion.4), channel_id=1, source_target_pairs={{0,4},{4,8},{8,12},{12,16},{16,20},{20,24},{24,28},{28,32},{32,36}... | collective-permute-start | bytes 196616 | tf_op jit(solution)/shard_map/while/body/eval_jaxpr/ppermute | solution.py:12
  59.2 29.6 %collective-permute-start = (f32[512,512]{1,0:T(8,128)}, f32[512,512]{1,0:T(8,128)}, u32[]{:S(2)}, u32[]{:S(2)}) collective-permute-start(f32[512,512]{1,0:T(8,128)} %get-tuple-element.404), channel_id=1, source_target_pairs={{0,4},{4,8},{8,12},{12,16},{16,20},{20,24},{24,28},{28,32},{32,36}... | collective-permute-start | bytes 3145736 | tf_op jit(solution)/shard_map/while/body/eval_jaxpr/ppermute | solution.py:12
  66.0 21.6 %collective-permute-start.1 = (f32[32,512]{1,0:T(8,128)S(1)}, f32[32,512]{1,0:T(8,128)S(1)}, u32[]{:S(2)}, u32[]{:S(2)}) collective-permute-start(f32[32,512]{1,0:T(8,128)S(1)} %broadcast_select_fusion.4), channel_id=1, source_target_pairs={{0,4},{4,8},{8,12},{12,16},{16,20},{20,24},{24,28},{28,32},{32,36}... | collective-permute-start | bytes 196616 | tf_op jit(solution)/shard_map/while/body/eval_jaxpr/ppermute | solution.py:12
  109.7 28.8 %collective-permute-start = (f32[512,512]{1,0:T(8,128)}, f32[512,512]{1,0:T(8,128)}, u32[]{:S(2)}, u32[]{:S(2)}) collective-permute-start(f32[512,512]{1,0:T(8,128)} %get-tuple-element.404), channel_id=1, source_target_pairs={{0,4},{4,8},{8,12},{12,16},{16,20},{20,24},{24,28},{28,32},{32,36}... | collective-permute-start | bytes 3145736 | tf_op jit(solution)/shard_map/while/body/eval_jaxpr/ppermute | solution.py:12
  116.5 20.9 %collective-permute-start.1 = (f32[32,512]{1,0:T(8,128)S(1)}, f32[32,512]{1,0:T(8,128)S(1)}, u32[]{:S(2)}, u32[]{:S(2)}) collective-permute-start(f32[32,512]{1,0:T(8,128)S(1)} %broadcast_select_fusion.4), channel_id=1, source_target_pairs={{0,4},{4,8},{8,12},{12,16},{16,20},{20,24},{24,28},{28,32},{32,36}... | collective-permute-start | bytes 196616 | tf_op jit(solution)/shard_map/while/body/eval_jaxpr/ppermute | solution.py:12
  159.5 28.1 %collective-permute-start = (f32[512,512]{1,0:T(8,128)}, f32[512,512]{1,0:T(8,128)}, u32[]{:S(2)}, u32[]{:S(2)}) collective-permute-start(f32[512,512]{1,0:T(8,128)} %get-tuple-element.404), channel_id=1, source_target_pairs={{0,4},{4,8},{8,12},{12,16},{16,20},{20,24},{24,28},{28,32},{32,36}... | collective-permute-start | bytes 3145736 | tf_op jit(solution)/shard_map/while/body/eval_jaxpr/ppermute | solution.py:12
  166.3 20.1 %collective-permute-start.1 = (f32[32,512]{1,0:T(8,128)S(1)}, f32[32,512]{1,0:T(8,128)S(1)}, u32[]{:S(2)}, u32[]{:S(2)}) collective-permute-start(f32[32,512]{1,0:T(8,128)S(1)} %broadcast_select_fusion.4), channel_id=1, source_target_pairs={{0,4},{4,8},{8,12},{12,16},{16,20},{20,24},{24,28},{28,32},{32,36}... | collective-permute-start | bytes 196616 | tf_op jit(solution)/shard_map/while/body/eval_jaxpr/ppermute | solution.py:12
  208.5 27.4 %collective-permute-start = (f32[512,512]{1,0:T(8,128)}, f32[512,512]{1,0:T(8,128)}, u32[]{:S(2)}, u32[]{:S(2)}) collective-permute-start(f32[512,512]{1,0:T(8,128)} %get-tuple-element.404), channel_id=1, source_target_pairs={{0,4},{4,8},{8,12},{12,16},{16,20},{20,24},{24,28},{28,32},{32,36}... | collective-permute-start | bytes 3145736 | tf_op jit(solution)/shard_map/while/body/eval_jaxpr/ppermute | solution.py:12
  215.4 19.4 collective-permute-start.1
  256.8 26.7 %collective-permute-start = (f32[512,512]{1,0:T(8,128)}, f32[512,512]{1,0:T(8,128)}, u32[]{:S(2)}, u32[]{:S(2)}) collective-permute-start(f32[512,512]{1,0:T(8,128)} %get-tuple-element.404), channel_id=1, source_target_pairs={{0,4},{4,8},{8,12},{12,16},{16,20},{20,24},{24,28},{28,32},{32,36}... | collective-permute-start | bytes 3145736 | tf_op jit(solution)/shard_map/while/body/eval_jaxpr/ppermute | solution.py:12
  264.0 18.4 collective-permute-start.1
  304.4 28.0 %collective-permute-start = (f32[512,512]{1,0:T(8,128)}, f32[512,512]{1,0:T(8,128)}, u32[]{:S(2)}, u32[]{:S(2)}) collective-permute-start(f32[512,512]{1,0:T(8,128)} %get-tuple-element.404), channel_id=1, source_target_pairs={{0,4},{4,8},{8,12},{12,16},{16,20},{20,24},{24,28},{28,32},{32,36}... | collective-permute-start | bytes 3145736 | tf_op jit(solution)/shard_map/while/body/eval_jaxpr/ppermute | solution.py:12
  313.6 17.6 collective-permute-start.1
  353.4 27.3 %collective-permute-start = (f32[512,512]{1,0:T(8,128)}, f32[512,512]{1,0:T(8,128)}, u32[]{:S(2)}, u32[]{:S(2)}) collective-permute-start(f32[512,512]{1,0:T(8,128)} %get-tuple-element.404), channel_id=1, source_target_pairs={{0,4},{4,8},{8,12},{12,16},{16,20},{20,24},{24,28},{28,32},{32,36}... | collective-permute-start | bytes 3145736 | tf_op jit(solution)/shard_map/while/body/eval_jaxpr/ppermute | solution.py:12
  362.6 16.9 collective-permute-start.1
  401.6 26.6 %collective-permute-start = (f32[512,512]{1,0:T(8,128)}, f32[512,512]{1,0:T(8,128)}, u32[]{:S(2)}, u32[]{:S(2)}) collective-permute-start(f32[512,512]{1,0:T(8,128)} %get-tuple-element.404), channel_id=1, source_target_pairs={{0,4},{4,8},{8,12},{12,16},{16,20},{20,24},{24,28},{28,32},{32,36}... | collective-permute-start | bytes 3145736 | tf_op jit(solution)/shard_map/while/body/eval_jaxpr/ppermute | solution.py:12
  410.8 16.1 collective-permute-start.1
  449.1 25.6 %collective-permute-start = (f32[512,512]{1,0:T(8,128)}, f32[512,512]{1,0:T(8,128)}, u32[]{:S(2)}, u32[]{:S(2)}) collective-permute-start(f32[512,512]{1,0:T(8,128)} %get-tuple-element.404), channel_id=1, source_target_pairs={{0,4},{4,8},{8,12},{12,16},{16,20},{20,24},{24,28},{28,32},{32,36}... | collective-permute-start | bytes 3145736 | tf_op jit(solution)/shard_map/while/body/eval_jaxpr/ppermute | solution.py:12
  458.2 15.4 collective-permute-start.1
  495.7 25.1 %collective-permute-start = (f32[512,512]{1,0:T(8,128)}, f32[512,512]{1,0:T(8,128)}, u32[]{:S(2)}, u32[]{:S(2)}) collective-permute-start(f32[512,512]{1,0:T(8,128)} %get-tuple-element.404), channel_id=1, source_target_pairs={{0,4},{4,8},{8,12},{12,16},{16,20},{20,24},{24,28},{28,32},{32,36}... | collective-permute-start | bytes 3145736 | tf_op jit(solution)/shard_map/while/body/eval_jaxpr/ppermute | solution.py:12
  505.0 14.6 collective-permute-start.1
  541.7 24.4 %collective-permute-start = (f32[512,512]{1,0:T(8,128)}, f32[512,512]{1,0:T(8,128)}, u32[]{:S(2)}, u32[]{:S(2)}) collective-permute-start(f32[512,512]{1,0:T(8,128)} %get-tuple-element.404), channel_id=1, source_target_pairs={{0,4},{4,8},{8,12},{12,16},{16,20},{20,24},{24,28},{28,32},{32,36}... | collective-permute-start | bytes 3145736 | tf_op jit(solution)/shard_map/while/body/eval_jaxpr/ppermute | solution.py:12
  551.0 13.9 collective-permute-start.1
  587.0 23.6 %collective-permute-start = (f32[512,512]{1,0:T(8,128)}, f32[512,512]{1,0:T(8,128)}, u32[]{:S(2)}, u32[]{:S(2)}) collective-permute-start(f32[512,512]{1,0:T(8,128)} %get-tuple-element.404), channel_id=1, source_target_pairs={{0,4},{4,8},{8,12},{12,16},{16,20},{20,24},{24,28},{28,32},{32,36}... | collective-permute-start | bytes 3145736 | tf_op jit(solution)/shard_map/while/body/eval_jaxpr/ppermute | solution.py:12
  596.3 13.2 collective-permute-start.1
  631.6 22.7 %collective-permute-start = (f32[512,512]{1,0:T(8,128)}, f32[512,512]{1,0:T(8,128)}, u32[]{:S(2)}, u32[]{:S(2)}) collective-permute-start(f32[512,512]{1,0:T(8,128)} %get-tuple-element.404), channel_id=1, source_target_pairs={{0,4},{4,8},{8,12},{12,16},{16,20},{20,24},{24,28},{28,32},{32,36}... | collective-permute-start | bytes 3145736 | tf_op jit(solution)/shard_map/while/body/eval_jaxpr/ppermute | solution.py:12
  640.8 12.4 collective-permute-start.1
  675.3 22.0 %collective-permute-start = (f32[512,512]{1,0:T(8,128)}, f32[512,512]{1,0:T(8,128)}, u32[]{:S(2)}, u32[]{:S(2)}) collective-permute-start(f32[512,512]{1,0:T(8,128)} %get-tuple-element.404), channel_id=1, source_target_pairs={{0,4},{4,8},{8,12},{12,16},{16,20},{20,24},{24,28},{28,32},{32,36}... | collective-permute-start | bytes 3145736 | tf_op jit(solution)/shard_map/while/body/eval_jaxpr/ppermute | solution.py:12
  718.2 21.9 %collective-permute-start = (f32[512,512]{1,0:T(8,128)}, f32[512,512]{1,0:T(8,128)}, u32[]{:S(2)}, u32[]{:S(2)}) collective-permute-start(f32[512,512]{1,0:T(8,128)} %get-tuple-element.404), channel_id=1, source_target_pairs={{0,4},{4,8},{8,12},{12,16},{16,20},{20,24},{24,28},{28,32},{32,36}... | collective-permute-start | bytes 3145736 | tf_op jit(solution)/shard_map/while/body/eval_jaxpr/ppermute | solution.py:12
  761.0 22.0 %collective-permute-start = (f32[512,512]{1,0:T(8,128)}, f32[512,512]{1,0:T(8,128)}, u32[]{:S(2)}, u32[]{:S(2)}) collective-permute-start(f32[512,512]{1,0:T(8,128)} %get-tuple-element.404), channel_id=1, source_target_pairs={{0,4},{4,8},{8,12},{12,16},{16,20},{20,24},{24,28},{28,32},{32,36}... | collective-permute-start | bytes 3145736 | tf_op jit(solution)/shard_map/while/body/eval_jaxpr/ppermute | solution.py:12
  804.0 21.8 %collective-permute-start = (f32[512,512]{1,0:T(8,128)}, f32[512,512]{1,0:T(8,128)}, u32[]{:S(2)}, u32[]{:S(2)}) collective-permute-start(f32[512,512]{1,0:T(8,128)} %get-tuple-element.404), channel_id=1, source_target_pairs={{0,4},{4,8},{8,12},{12,16},{16,20},{20,24},{24,28},{28,32},{32,36}... | collective-permute-start | bytes 3145736 | tf_op jit(solution)/shard_map/while/body/eval_jaxpr/ppermute | solution.py:12
  846.7 21.7 %collective-permute-start = (f32[512,512]{1,0:T(8,128)}, f32[512,512]{1,0:T(8,128)}, u32[]{:S(2)}, u32[]{:S(2)}) collective-permute-start(f32[512,512]{1,0:T(8,128)} %get-tuple-element.404), channel_id=1, source_target_pairs={{0,4},{4,8},{8,12},{12,16},{16,20},{20,24},{24,28},{28,32},{32,36}... | collective-permute-start | bytes 3145736 | tf_op jit(solution)/shard_map/while/body/eval_jaxpr/ppermute | solution.py:12
  889.4 21.6 %collective-permute-start = (f32[512,512]{1,0:T(8,128)}, f32[512,512]{1,0:T(8,128)}, u32[]{:S(2)}, u32[]{:S(2)}) collective-permute-start(f32[512,512]{1,0:T(8,128)} %get-tuple-element.404), channel_id=1, source_target_pairs={{0,4},{4,8},{8,12},{12,16},{16,20},{20,24},{24,28},{28,32},{32,36}... | collective-permute-start | bytes 3145736 | tf_op jit(solution)/shard_map/while/body/eval_jaxpr/ppermute | solution.py:12
  931.9 22.8 %collective-permute-start = (f32[512,512]{1,0:T(8,128)}, f32[512,512]{1,0:T(8,128)}, u32[]{:S(2)}, u32[]{:S(2)}) collective-permute-start(f32[512,512]{1,0:T(8,128)} %get-tuple-element.404), channel_id=1, source_target_pairs={{0,4},{4,8},{8,12},{12,16},{16,20},{20,24},{24,28},{28,32},{32,36}... | collective-permute-start | bytes 3145736 | tf_op jit(solution)/shard_map/while/body/eval_jaxpr/ppermute | solution.py:12
  975.6 22.7 %collective-permute-start = (f32[512,512]{1,0:T(8,128)}, f32[512,512]{1,0:T(8,128)}, u32[]{:S(2)}, u32[]{:S(2)}) collective-permute-start(f32[512,512]{1,0:T(8,128)} %get-tuple-element.404), channel_id=1, source_target_pairs={{0,4},{4,8},{8,12},{12,16},{16,20},{20,24},{24,28},{28,32},{32,36}... | collective-permute-start | bytes 3145736 | tf_op jit(solution)/shard_map/while/body/eval_jaxpr/ppermute | solution.py:12
  1019.2 22.5 %collective-permute-start = (f32[512,512]{1,0:T(8,128)}, f32[512,512]{1,0:T(8,128)}, u32[]{:S(2)}, u32[]{:S(2)}) collective-permute-start(f32[512,512]{1,0:T(8,128)} %get-tuple-element.404), channel_id=1, source_target_pairs={{0,4},{4,8},{8,12},{12,16},{16,20},{20,24},{24,28},{28,32},{32,36}... | collective-permute-start | bytes 3145736 | tf_op jit(solution)/shard_map/while/body/eval_jaxpr/ppermute | solution.py:12
  1062.7 22.2 %collective-permute-start = (f32[512,512]{1,0:T(8,128)}, f32[512,512]{1,0:T(8,128)}, u32[]{:S(2)}, u32[]{:S(2)}) collective-permute-start(f32[512,512]{1,0:T(8,128)} %get-tuple-element.404), channel_id=1, source_target_pairs={{0,4},{4,8},{8,12},{12,16},{16,20},{20,24},{24,28},{28,32},{32,36}... | collective-permute-start | bytes 3145736 | tf_op jit(solution)/shard_map/while/body/eval_jaxpr/ppermute | solution.py:12
  1105.8 22.2 %collective-permute-start = (f32[512,512]{1,0:T(8,128)}, f32[512,512]{1,0:T(8,128)}, u32[]{:S(2)}, u32[]{:S(2)}) collective-permute-start(f32[512,512]{1,0:T(8,128)} %get-tuple-element.404), channel_id=1, source_target_pairs={{0,4},{4,8},{8,12},{12,16},{16,20},{20,24},{24,28},{28,32},{32,36}... | collective-permute-start | bytes 3145736 | tf_op jit(solution)/shard_map/while/body/eval_jaxpr/ppermute | solution.py:12
  1148.9 22.2 %collective-permute-start = (f32[512,512]{1,0:T(8,128)}, f32[512,512]{1,0:T(8,128)}, u32[]{:S(2)}, u32[]{:S(2)}) collective-permute-start(f32[512,512]{1,0:T(8,128)} %get-tuple-element.404), channel_id=1, source_target_pairs={{0,4},{4,8},{8,12},{12,16},{16,20},{20,24},{24,28},{28,32},{32,36}... | collective-permute-start | bytes 3145736 | tf_op jit(solution)/shard_map/while/body/eval_jaxpr/ppermute | solution.py:12
  1192.0 22.2 %collective-permute-start = (f32[512,512]{1,0:T(8,128)}, f32[512,512]{1,0:T(8,128)}, u32[]{:S(2)}, u32[]{:S(2)}) collective-permute-start(f32[512,512]{1,0:T(8,128)} %get-tuple-element.404), channel_id=1, source_target_pairs={{0,4},{4,8},{8,12},{12,16},{16,20},{20,24},{24,28},{28,32},{32,36}... | collective-permute-start | bytes 3145736 | tf_op jit(solution)/shard_map/while/body/eval_jaxpr/ppermute | solution.py:12
  1235.1 22.2 %collective-permute-start = (f32[512,512]{1,0:T(8,128)}, f32[512,512]{1,0:T(8,128)}, u32[]{:S(2)}, u32[]{:S(2)}) collective-permute-start(f32[512,512]{1,0:T(8,128)} %get-tuple-element.404), channel_id=1, source_target_pairs={{0,4},{4,8},{8,12},{12,16},{16,20},{20,24},{24,28},{28,32},{32,36}... | collective-permute-start | bytes 3145736 | tf_op jit(solution)/shard_map/while/body/eval_jaxpr/ppermute | solution.py:12
  1278.3 22.2 %collective-permute-start = (f32[512,512]{1,0:T(8,128)}, f32[512,512]{1,0:T(8,128)}, u32[]{:S(2)}, u32[]{:S(2)}) collective-permute-start(f32[512,512]{1,0:T(8,128)} %get-tuple-element.404), channel_id=1, source_target_pairs={{0,4},{4,8},{8,12},{12,16},{16,20},{20,24},{24,28},{28,32},{32,36}... | collective-permute-start | bytes 3145736 | tf_op jit(solution)/shard_map/while/body/eval_jaxpr/ppermute | solution.py:12
  1321.4 22.2 %collective-permute-start = (f32[512,512]{1,0:T(8,128)}, f32[512,512]{1,0:T(8,128)}, u32[]{:S(2)}, u32[]{:S(2)}) collective-permute-start(f32[512,512]{1,0:T(8,128)} %get-tuple-element.404), channel_id=1, source_target_pairs={{0,4},{4,8},{8,12},{12,16},{16,20},{20,24},{24,28},{28,32},{32,36}... | collective-permute-start | bytes 3145736 | tf_op jit(solution)/shard_map/while/body/eval_jaxpr/ppermute | solution.py:12
  1364.5 22.2 %collective-permute-start = (f32[512,512]{1,0:T(8,128)}, f32[512,512]{1,0:T(8,128)}, u32[]{:S(2)}, u32[]{:S(2)}) collective-permute-start(f32[512,512]{1,0:T(8,128)} %get-tuple-element.404), channel_id=1, source_target_pairs={{0,4},{4,8},{8,12},{12,16},{16,20},{20,24},{24,28},{28,32},{32,36}... | collective-permute-start | bytes 3145736 | tf_op jit(solution)/shard_map/while/body/eval_jaxpr/ppermute | solution.py:12
  1407.6 22.2 %collective-permute-start = (f32[512,512]{1,0:T(8,128)}, f32[512,512]{1,0:T(8,128)}, u32[]{:S(2)}, u32[]{:S(2)}) collective-permute-start(f32[512,512]{1,0:T(8,128)} %get-tuple-element.404), channel_id=1, source_target_pairs={{0,4},{4,8},{8,12},{12,16},{16,20},{20,24},{24,28},{28,32},{32,36}... | collective-permute-start | bytes 3145736 | tf_op jit(solution)/shard_map/while/body/eval_jaxpr/ppermute | solution.py:12
  1450.7 22.2 %collective-permute-start = (f32[512,512]{1,0:T(8,128)}, f32[512,512]{1,0:T(8,128)}, u32[]{:S(2)}, u32[]{:S(2)}) collective-permute-start(f32[512,512]{1,0:T(8,128)} %get-tuple-element.404), channel_id=1, source_target_pairs={{0,4},{4,8},{8,12},{12,16},{16,20},{20,24},{24,28},{28,32},{32,36}... | collective-permute-start | bytes 3145736 | tf_op jit(solution)/shard_map/while/body/eval_jaxpr/ppermute | solution.py:12
  (55 other events, 2326.6 us)
Sparse Core Ops, SparseCore 0:
  1496.2 356.0 all-reduce.2
where the time goes:
time: 1970 us; the launch traced here: 1960 us
  waiting for transfers between devices  553 us (28%)
  other arithmetic  467 us (24%)
  starting transfers between devices  465 us (24%)
  matrix products  264 us (13%)
  local copies, waits for them, and re-layouts  164 us (8%)
  blocking collectives  28.3 us (1%)
    ppermute x66, starting transfers between devices, from_behind(): lax.ppermute(value, axis, [(source, source + steps) for source in range(f...  465 us
    psum x1, waiting for transfers between devices, from_root(): return lax.psum(block, axis)  356 us
    dot_general x165, matrix products, product(): jnp.dot(left, right, precision=lax.Precision.HIGHEST, preferred_element_t...  241 us
    another operation x99, other arithmetic, woodbury(): factor = jnp.linalg.cholesky(system)  240 us
    ppermute x66, waiting for transfers between devices, from_behind(): lax.ppermute(value, axis, [(source, source + steps) for source in range(f...  198 us
    another operation x66, other arithmetic, woodbury(): gain_rows = jax.scipy.linalg.cho_solve((factor, True), cross_term.T)  183 us
    psum x2, local copies, waits for them, and re-layouts, from_root(): return lax.psum(block, axis)  61.3 us
    dynamic_slice x33, local copies, waits for them, and re-layouts, one_turn(): old_est = lax.dynamic_index_in_dim(kept_est, clipped, 0, keepdims=False)  48.5 us
  transfers between devices with their start and end apart: 67, of which 34 were waited for; matrix products, arithmetic and copies ran while one was open for 7% of the time, Pallas kernels for 0%

commit v1 on v0

--- a/solution.py
+++ b/solution.py
@@ -4,6 +4,12 @@
 from jax.sharding import PartitionSpec as P
 
 prior_var = 0.1
+
+
+def add_all(shard, mesh_axis):
+    pieces = lax.all_gather(shard, mesh_axis, axis=0, tiled=False)
+    summed = pieces.sum(axis=0)
+    return summed
 
 
 def from_behind(value, axis, steps):
@@ -14,7 +20,7 @@
 
 def from_root(block, axis, source):
     block = jnp.where(lax.axis_index(axis) == source, block, jnp.zeros_like(block))
-    return lax.psum(block, axis)
+    return add_all(block, axis)
 
 
 def product(left, right):

time: 1970 us -> 2550 us (1.29)
  waiting for transfers between devices: 553 us -> 1100 us
  other arithmetic: 467 us -> 518 us
    all_gather x0 -> x2, waiting for transfers between devices: none -> 927 us  [add_all(): pieces = lax.all_gather(shard, mesh_axis, axis=0, tiled=False)]
    psum x1 -> x0, waiting for transfers between devices: 356 us -> none  [from_root(): return lax.psum(block, axis)]
    psum x2 -> x0, local copies, waits for them, and re-layouts: 61.3 us -> none  [from_root(): return lax.psum(block, axis)]
    reduce_sum x0 -> x2, local copies, waits for them, and re-layouts: none -> 59.7 us  [add_all(): summed = pieces.sum(axis=0)]
    ppermute x66, waiting for transfers between devices: 198 us -> 170 us  [from_behind(): lax.ppermute(value, axis, [(source, source + steps) for source in range(f...]
    while x33, other arithmetic: 0.24 us -> 27.1 us
  transfers between devices with their start and end apart: 67 -> 68, of which waited for: 34 -> 35; matrix products, arithmetic and copies ran while one was open for 7% -> 6% of each run, Pallas kernels for 0% -> 0%
where the time goes in v1:
time: 2550 us; the launch traced here: 2530 us
  waiting for transfers between devices  1100 us (43%)
  other arithmetic  518 us (20%)
  starting transfers between devices  465 us (18%)
  matrix products  265 us (10%)
  local copies, waits for them, and re-layouts  163 us (6%)
    all_gather x2, waiting for transfers between devices, add_all(): pieces = lax.all_gather(shard, mesh_axis, axis=0, tiled=False)  927 us
    ppermute x66, starting transfers between devices, from_behind(): lax.ppermute(value, axis, [(source, source + steps) for source in range(f...  465 us
    dot_general x165, matrix products, product(): jnp.dot(left, right, precision=lax.Precision.HIGHEST, preferred_element_t...  242 us
    another operation x99, other arithmetic, woodbury(): factor = jnp.linalg.cholesky(system)  240 us
    another operation x66, other arithmetic, woodbury(): gain_rows = jax.scipy.linalg.cho_solve((factor, True), cross_term.T)  183 us
    ppermute x66, waiting for transfers between devices, from_behind(): lax.ppermute(value, axis, [(source, source + steps) for source in range(f...  170 us
    reduce_sum x2, local copies, waits for them, and re-layouts, add_all(): summed = pieces.sum(axis=0)  59.7 us
  transfers between devices with their start and end apart: 68, of which 35 were waited for; matrix products, arithmetic and copies ran while one was open for 6% of the time, Pallas kernels for 0%

profile of v1, /device:TPU:1, one launch (start us, length us, event | category | flops | bytes accessed | tf_op | source)
XLA Modules:
  0.0 2534.0 jit_solution(9312097905576407171)
XLA Ops:
  9.3 1486.9 %while.21 = (s32[]{:T(128)}, f32[512,512]{1,0:T(8,128)}, f32[32,512]{1,0:T(8,128)}, f32[2,512,512]{2,1,0:T(8,128)S(1)}, f32[2,32,512]{2,1,0:T(8,128)}, /*index=5...) while((s32[]{:T(128)}, f32[512,512]{1,0:T(8,128)}, ...), condition=%wide.region_3.4_spmd.clone, body=%wide.region_0.3_spmd.clone.sunk | while | flops 505559104 | bytes 14437732 | solution.py:87
  20.1 17.0 collective-permute-done.1
  59.2 6.8 collective-permute-start
  72.2 15.5 collective-permute-done.1
  93.5 6.6 cholesky.65
  109.9 6.8 collective-permute-start
  122.9 14.7 collective-permute-done.1
  159.7 6.8 collective-permute-start
  172.7 14.0 collective-permute-done.1
  208.9 6.8 collective-permute-start
  223.0 12.1 collective-permute-done.1
  257.2 7.1 collective-permute-start
  273.6 9.2 collective-permute-done.1
  304.9 9.3 collective-permute-start
  323.4 8.5 collective-permute-done.1
  354.1 9.2 collective-permute-start
  372.4 7.7 collective-permute-done.1
  402.3 9.2 collective-permute-start
  420.7 7.0 collective-permute-done.1
  449.8 9.3 collective-permute-start
  496.6 9.2 collective-permute-start
  542.6 9.3 collective-permute-start
  588.0 9.2 collective-permute-start
  632.5 9.2 collective-permute-start
  676.3 9.3 collective-permute-start
  719.3 9.1 collective-permute-start
  762.2 9.3 collective-permute-start
  805.3 9.0 collective-permute-start
  848.0 8.9 collective-permute-start
  890.7 8.9 collective-permute-start
  933.3 10.0 collective-permute-start
  977.1 9.9 collective-permute-start
  1020.8 9.8 collective-permute-start
  1064.4 9.4 collective-permute-start
  1107.6 9.4 collective-permute-start
  1150.7 9.4 collective-permute-start
  1193.9 9.4 collective-permute-start
  1237.1 9.4 collective-permute-start
  1280.3 9.4 collective-permute-start
  1323.4 9.4 collective-permute-start
  1366.6 9.4 collective-permute-start
  1409.8 9.4 collective-permute-start
  1453.0 9.4 collective-permute-start
  1499.1 196.6 %all-gather.7.cloned.1.call-done = f32[64,32,512]{2,1,0:T(8,128)} async-done(((f32[2,32,512]{2,1,0:T(8,128)}), f32[64,32,512]{2,1,0:T(8,128)}) %all-gather.7.cloned.1.call-update) | async-done | bytes 4194320 | tf_op jit(solution)/shard_map/all_gather | solution.py:10
  1699.9 730.6 %all-gather.5.cloned.1.call-done = f32[64,512,512]{2,1,0:T(8,128)} async-done(((f32[2,512,512]{2,1,0:T(8,128)}), f32[64,512,512]{2,1,0:T(8,128)}) %all-gather.5.cloned.1.call-update) | async-done | bytes 67108880 | tf_op jit(solution)/shard_map/all_gather | solution.py:10
  2430.5 20.9 reduce_sum.27
  2451.4 59.5 %copy.11 = f32[2,512,512]{0,2,1:T(8,128)} copy(f32[2,512,512]{2,1,0:T(8,128)S(1)} %reduce_sum.27) | data formatting | bytes 4194304 | tf_op jit(solution)/shard_map/reduce_sum | solution.py:11
  2516.5 7.4 psum.7
  (778 shorter events, 1102.6 us)
Async XLA Ops:
  7.2 1688.6 %all-gather.7.cloned.1.call-start = ((), (), s32[]{:S(2)}) async-start(), calls=%async_computation.1 | async-start | bytes 4325376 | tf_op jit(solution)/shard_map/all_gather | solution.py:10
  9.3 29.0 %collective-permute-start = (f32[512,512]{1,0:T(8,128)}, f32[512,512]{1,0:T(8,128)}, u32[]{:S(2)}, u32[]{:S(2)}) collective-permute-start(f32[512,512]{1,0:T(8,128)} %get-tuple-element.380), channel_id=1, source_target_pairs={{0,4},{4,8},{8,12},{12,16},{16,20},{20,24},{24,28},{28,32},{32,36}... | collective-permute-start | bytes 3145736 | tf_op jit(solution)/shard_map/while/body/eval_jaxpr/ppermute | solution.py:18
  14.7 22.4 collective-permute-start.1
  59.2 29.6 %collective-permute-start = (f32[512,512]{1,0:T(8,128)}, f32[512,512]{1,0:T(8,128)}, u32[]{:S(2)}, u32[]{:S(2)}) collective-permute-start(f32[512,512]{1,0:T(8,128)} %get-tuple-element.380), channel_id=1, source_target_pairs={{0,4},{4,8},{8,12},{12,16},{16,20},{20,24},{24,28},{28,32},{32,36}... | collective-permute-start | bytes 3145736 | tf_op jit(solution)/shard_map/while/body/eval_jaxpr/ppermute | solution.py:18
  66.9 20.8 collective-permute-start.1
  109.9 28.9 %collective-permute-start = (f32[512,512]{1,0:T(8,128)}, f32[512,512]{1,0:T(8,128)}, u32[]{:S(2)}, u32[]{:S(2)}) collective-permute-start(f32[512,512]{1,0:T(8,128)} %get-tuple-element.380), channel_id=1, source_target_pairs={{0,4},{4,8},{8,12},{12,16},{16,20},{20,24},{24,28},{28,32},{32,36}... | collective-permute-start | bytes 3145736 | tf_op jit(solution)/shard_map/while/body/eval_jaxpr/ppermute | solution.py:18
  117.5 20.1 collective-permute-start.1
  159.7 28.1 %collective-permute-start = (f32[512,512]{1,0:T(8,128)}, f32[512,512]{1,0:T(8,128)}, u32[]{:S(2)}, u32[]{:S(2)}) collective-permute-start(f32[512,512]{1,0:T(8,128)} %get-tuple-element.380), channel_id=1, source_target_pairs={{0,4},{4,8},{8,12},{12,16},{16,20},{20,24},{24,28},{28,32},{32,36}... | collective-permute-start | bytes 3145736 | tf_op jit(solution)/shard_map/while/body/eval_jaxpr/ppermute | solution.py:18
  167.4 19.3 collective-permute-start.1
  208.9 27.4 %collective-permute-start = (f32[512,512]{1,0:T(8,128)}, f32[512,512]{1,0:T(8,128)}, u32[]{:S(2)}, u32[]{:S(2)}) collective-permute-start(f32[512,512]{1,0:T(8,128)} %get-tuple-element.380), channel_id=1, source_target_pairs={{0,4},{4,8},{8,12},{12,16},{16,20},{20,24},{24,28},{28,32},{32,36}... | collective-permute-start | bytes 3145736 | tf_op jit(solution)/shard_map/while/body/eval_jaxpr/ppermute | solution.py:18
  216.5 18.6 collective-permute-start.1
  257.2 26.7 %collective-permute-start = (f32[512,512]{1,0:T(8,128)}, f32[512,512]{1,0:T(8,128)}, u32[]{:S(2)}, u32[]{:S(2)}) collective-permute-start(f32[512,512]{1,0:T(8,128)} %get-tuple-element.380), channel_id=1, source_target_pairs={{0,4},{4,8},{8,12},{12,16},{16,20},{20,24},{24,28},{28,32},{32,36}... | collective-permute-start | bytes 3145736 | tf_op jit(solution)/shard_map/while/body/eval_jaxpr/ppermute | solution.py:18
  265.2 17.5 collective-permute-start.1
  304.9 28.1 %collective-permute-start = (f32[512,512]{1,0:T(8,128)}, f32[512,512]{1,0:T(8,128)}, u32[]{:S(2)}, u32[]{:S(2)}) collective-permute-start(f32[512,512]{1,0:T(8,128)} %get-tuple-element.380), channel_id=1, source_target_pairs={{0,4},{4,8},{8,12},{12,16},{16,20},{20,24},{24,28},{28,32},{32,36}... | collective-permute-start | bytes 3145736 | tf_op jit(solution)/shard_map/while/body/eval_jaxpr/ppermute | solution.py:18
  315.1 16.8 collective-permute-start.1
  354.1 27.2 %collective-permute-start = (f32[512,512]{1,0:T(8,128)}, f32[512,512]{1,0:T(8,128)}, u32[]{:S(2)}, u32[]{:S(2)}) collective-permute-start(f32[512,512]{1,0:T(8,128)} %get-tuple-element.380), channel_id=1, source_target_pairs={{0,4},{4,8},{8,12},{12,16},{16,20},{20,24},{24,28},{28,32},{32,36}... | collective-permute-start | bytes 3145736 | tf_op jit(solution)/shard_map/while/body/eval_jaxpr/ppermute | solution.py:18
  364.1 16.1 collective-permute-start.1
  402.3 26.5 %collective-permute-start = (f32[512,512]{1,0:T(8,128)}, f32[512,512]{1,0:T(8,128)}, u32[]{:S(2)}, u32[]{:S(2)}) collective-permute-start(f32[512,512]{1,0:T(8,128)} %get-tuple-element.380), channel_id=1, source_target_pairs={{0,4},{4,8},{8,12},{12,16},{16,20},{20,24},{24,28},{28,32},{32,36}... | collective-permute-start | bytes 3145736 | tf_op jit(solution)/shard_map/while/body/eval_jaxpr/ppermute | solution.py:18
  412.4 15.3 collective-permute-start.1
  449.8 25.8 %collective-permute-start = (f32[512,512]{1,0:T(8,128)}, f32[512,512]{1,0:T(8,128)}, u32[]{:S(2)}, u32[]{:S(2)}) collective-permute-start(f32[512,512]{1,0:T(8,128)} %get-tuple-element.380), channel_id=1, source_target_pairs={{0,4},{4,8},{8,12},{12,16},{16,20},{20,24},{24,28},{28,32},{32,36}... | collective-permute-start | bytes 3145736 | tf_op jit(solution)/shard_map/while/body/eval_jaxpr/ppermute | solution.py:18
  459.9 14.5 collective-permute-start.1
  496.6 25.0 collective-permute-start
  506.7 13.8 collective-permute-start.1
  542.6 24.3 collective-permute-start
  552.8 13.1 collective-permute-start.1
  588.0 23.5 collective-permute-start
  598.0 12.3 collective-permute-start.1
  632.5 22.8 collective-permute-start
  676.3 22.1 collective-permute-start
  719.3 21.9 collective-permute-start
  762.2 22.0 collective-permute-start
  805.3 21.8 collective-permute-start
  848.0 21.7 collective-permute-start
  890.7 21.6 collective-permute-start
  933.3 22.8 collective-permute-start
  977.1 22.7 collective-permute-start
  1020.8 22.6 collective-permute-start
  1064.4 22.2 collective-permute-start
  1107.6 22.2 collective-permute-start
  1150.7 22.2 collective-permute-start
  1193.9 22.2 collective-permute-start
  1237.1 22.2 collective-permute-start
  1280.3 22.2 collective-permute-start
  1323.4 22.2 collective-permute-start
  1366.6 22.2 collective-permute-start
  1409.8 22.2 collective-permute-start
  1453.0 22.2 collective-permute-start
  1496.8 933.6 %all-gather.5.cloned.1.call-start = ((), (), s32[]{:S(2)}) async-start(), calls=%async_computation | async-start | bytes 69206016 | tf_op jit(solution)/shard_map/all_gather | solution.py:10
  (55 other events, 2803.0 us)
Sparse Core Ops, SparseCore 0:
  1497.0 198.7 all-gather.6
  1697.4 732.9 all-gather.4
